TPU v7x, 32 devices: a whole 2x2x4 slice. The times are simulated.
32 devices in a mesh: ha: 2 (over y), wa: 16 (over z, x, core).
Axes of the slice: x: 2, y: 2, z: 4, core: 2. Of those that a mesh axis runs over, the one named last changes fastest.
Arguments:
- block_input: bfloat16 [3, 46, 160, 128], P(None, 'ha', 'wa'), may hold values from -6 to 6
- cotangent: bfloat16 [3, 46, 160, 128], P(None, 'ha', 'wa'), may hold values from -6 to 6
- kernel_one: bfloat16 [3, 3, 3, 128, 128], replicated, may hold values from -0.109375 to 0.109375
- bias_one: float32 [128], replicated, may hold values from -3 to 3
- kernel_two: bfloat16 [3, 3, 3, 128, 128], replicated, may hold values from -0.109375 to 0.109375
- scale_one: float32 [128], replicated, may hold values from 0.5 to 2
- shift_one: float32 [128], replicated, may hold values from -1 to 1
- scale_two: float32 [128], replicated, may hold values from 0.5 to 2
- shift_two: float32 [128], replicated, may hold values from -1 to 1
Outputs:
- grad_input: bfloat16 [3, 46, 160, 128], P(None, 'ha', 'wa')
- grad_kernel_one: float32 [3, 3, 3, 128, 128], replicated
- grad_bias_one: float32 [128], replicated
- grad_kernel_two: float32 [3, 3, 3, 128, 128], replicated
- grad_bias_two: float32 [128], replicated
All inputs are finite; a program needn't handle non-finite values.
Results may differ from a plain program's by a relative error of at most 0.0054.
Values may be sent and summed in bfloat16 or wider, within the bound.
A program may use at most 64 MiB of HBM per device.

v0:
```python
import math

import jax
import jax.numpy as jnp
from jax import lax
from jax.sharding import PartitionSpec as P


def with_halo(cells, sides, width):
    for axis, dim in sides:
        count = lax.axis_size(axis)
        ends = count - 1
        head = lax.slice_in_dim(cells, 0, width, axis=dim)
        tail = lax.slice_in_dim(cells, cells.shape[dim] - width, cells.shape[dim], axis=dim)
        cells = jnp.concatenate(
            [
                lax.ppermute(tail, axis, [(i, (i + 1) % count) for i in range(ends)]),
                cells,
                lax.ppermute(head, axis, [((i + 1) % count, i) for i in range(ends)]),
            ],
            axis=dim,
        )
    return cells


def slope(value):
    sigma = jax.nn.sigmoid(value)
    return sigma * (1.0 + value * (1.0 - sigma))


def widen(padded, columns):
    return jnp.concatenate([padded[:, :, shift : shift + columns] for shift in range(3)], axis=-1)


def convolve(wide, kernel, frames, rows):
    columns = wide.shape[2]
    inner = kernel.shape[3]
    total = jnp.zeros((frames * rows * columns, kernel.shape[4]), jnp.float32)
    for step_t in range(3):
        for step_h in range(3):
            slab = wide[step_t : step_t + frames, step_h : step_h + rows].reshape(-1, 3 * inner)
            total = total + jnp.dot(
                slab,
                kernel[step_t, step_h].reshape(3 * inner, -1),
                preferred_element_type=jnp.float32,
            )
    return total.reshape(frames, rows, columns, -1)


def kernel_terms(wide, grads, frames, rows):
    inner = wide.shape[3] // 3
    pieces = []
    for step_t in range(3):
        for step_h in range(3):
            slab = wide[step_t : step_t + frames, step_h : step_h + rows].reshape(-1, 3 * inner)
            pieces.append(
                lax.dot_general(
                    slab, grads, (((0,), (0,)), ((), ())), preferred_element_type=jnp.float32
                )
            )
    return jnp.stack(pieces).reshape(3, 3, 3, inner, grads.shape[1])


def flipped(kernel):
    return jnp.transpose(kernel[::-1, ::-1, ::-1], (0, 1, 2, 4, 3))


def body(
    block_input,
    cotangent,
    kernel_one,
    bias_one,
    kernel_two,
    scale_one,
    shift_one,
    scale_two,
    shift_two,
):
    frames, rows, columns, chans = block_input.shape
    factor = 1.0 / math.sqrt(frames * rows * lax.axis_size("ha") * columns * lax.axis_size("wa"))
    front = ((2, 0), (0, 0), (0, 0), (0, 0))
    back = ((0, 2), (0, 0), (0, 0), (0, 0))
    first_pre = block_input.astype(jnp.float32) * scale_one + shift_one
    first_act = jax.nn.silu(first_pre).astype(jnp.bfloat16)
    joined = with_halo(jnp.stack([first_act, cotangent]), (("ha", 2), ("wa", 3)), 1)
    first_rim = joined[0]
    cot_halo = joined[1]
    first_wide = widen(jnp.pad(first_rim, front), columns)
    hidden = convolve(first_wide, kernel_one, frames, rows) + bias_one
    second_pre = hidden * scale_two + shift_two
    second_act = jax.nn.silu(second_pre).astype(jnp.bfloat16)
    second_rim = with_halo(second_act, (("ha", 1), ("wa", 2)), 1)
    second_wide = widen(jnp.pad(second_rim, front), columns)
    upstream = cotangent.reshape(-1, chans)
    grad_two = kernel_terms(second_wide, upstream, frames, rows)
    bias_b = jnp.sum(cotangent.astype(jnp.float32), axis=(0, 1, 2))
    cot_wide = widen(jnp.pad(cot_halo, back), columns)
    back_two = convolve(cot_wide, flipped(kernel_two), frames, rows)
    inner = (back_two * slope(second_pre) * scale_two).astype(jnp.bfloat16)
    inner_rim = with_halo(inner, (("ha", 1), ("wa", 2)), 1)
    inner_wide = widen(jnp.pad(inner_rim, back), columns)
    back_one = convolve(inner_wide, flipped(kernel_one), frames, rows)
    grad_input = (cotangent.astype(jnp.float32) + back_one * slope(first_pre) * scale_one).astype(
        jnp.bfloat16
    )
    grad_one = kernel_terms(first_wide, inner.reshape(-1, chans), frames, rows)
    bias_a = jnp.sum(inner.astype(jnp.float32), axis=(0, 1, 2))
    grad_one, bias_a, grad_two, bias_b = lax.psum(
        (grad_one, bias_a, grad_two, bias_b), ("ha", "wa")
    )
    return (grad_input, grad_one * factor, bias_a * factor, grad_two * factor, bias_b * factor)


def solution(mesh):
    return jax.shard_map(
        body,
        mesh=mesh,
        in_specs=(
            P(None, "ha", "wa", None),
            P(None, "ha", "wa", None),
            P(),
            P(),
            P(),
            P(),
            P(),
            P(),
            P(),
        ),
        out_specs=(P(None, "ha", "wa", None), P(), P(), P(), P()),
        check_vma=False,
    )
```

profile of v0, /device:TPU:0, one launch (start us, length us, event | category | flops | bytes accessed | tf_op | source)
XLA Modules:
  0.0 281.3 jit_solution(7883911846606421409)
XLA Ops:
  7.2 1.1 fusion.51
  9.3 4.9 %collective-permute-start = (bf16[2,3,1,10,128]{4,2,3,1,0:T(2,128)(2,1)S(1)}, bf16[2,3,1,10,128]{4,2,3,1,0:T(2,128)(2,1)S(1)}, u32[]{:S(2)}, u32[]{:S(2)}) collective-permute-start(bf16[2,3,1,10,128]{4,2,3,1,0:T(2,128)(2,1)S(1)} %get-tuple-element.75), channel_id=1, source_target_pairs={{0,16},{1,17},{2,18},{3,19},{4,20},{5,21},{6,22},{7,23},{8,24},{9,... | collective-permute-start | bytes 46088 | tf_op jit(solution)/shard_map/ppermute | solution.py:17
  14.2 1.3 collective-permute-start.1
  15.5 2.2 fusion.65
  17.7 1.4 copy.39
  19.0 2.0 copy.18
  22.3 1.5 collective-permute-start.2
  23.7 1.3 collective-permute-start.3
  26.0 2.5 collective-permute-done.3
  28.7 1.3 pad_slice_fusion.2
  30.2 1.9 fusion.63
  33.3 1.2 copy.19
  35.4 1.2 copy.20
  37.6 1.2 copy.21
  39.8 1.2 copy.22
  45.3 1.4 pad_maximum_fusion.1
  46.6 2.3 fusion.62
  50.1 1.2 copy.28
  52.3 1.2 copy.29
  54.5 1.2 copy.30
  56.6 1.2 copy.31
  58.8 1.2 copy.32
  61.0 1.2 copy.33
  63.1 1.2 copy.34
  67.6 1.3 fusion.72
  69.0 1.3 convolution_add_fusion.15
  73.3 1.3 fusion.71
  74.6 1.5 convolution_add_fusion.23
  79.6 4.5 %collective-permute-start.4 = (bf16[3,1,10,128]{3,1,2,0:T(2,128)(2,1)S(1)}, bf16[3,1,10,128]{3,1,2,0:T(2,128)(2,1)S(1)}, u32[]{:S(2)}, u32[]{:S(2)}) collective-permute-start(bf16[3,1,10,128]{3,1,2,0:T(2,128)(2,1)S(1)} %get-tuple-element.91), channel_id=1, source_target_pairs={{0,16},{1,17},{2,18},{3,19},{4,20},{5,21},{6,22},{7,23},{8,24},{9,... | collective-permute-start | bytes 23048 | tf_op jit(solution)/shard_map/ppermute | solution.py:17
  84.1 1.3 collective-permute-start.5
  85.5 4.5 %collective-permute-start.8 = (bf16[3,1,10,128]{3,1,2,0:T(2,128)(2,1)S(1)}, bf16[3,1,10,128]{3,1,2,0:T(2,128)(2,1)S(1)}, u32[]{:S(2)}, u32[]{:S(2)}) collective-permute-start(bf16[3,1,10,128]{3,1,2,0:T(2,128)(2,1)S(1)} %get-tuple-element.89), channel_id=1, source_target_pairs={{0,16},{1,17},{2,18},{3,19},{4,20},{5,21},{6,22},{7,23},{8,24},{9,... | collective-permute-start | bytes 23048 | tf_op jit(solution)/shard_map/ppermute | solution.py:17
  90.0 1.3 collective-permute-start.9
  94.3 3.9 %collective-permute-start.6 = (bf16[3,25,1,128]{3,1,2,0:T(8,128)(2,1)S(1)}, bf16[3,25,1,128]{3,1,2,0:T(8,128)(2,1)S(1)}, u32[]{:S(2)}, u32[]{:S(2)}) collective-permute-start(bf16[3,25,1,128]{3,1,2,0:T(8,128)(2,1)S(1)} %get-tuple-element.85), channel_id=1, source_target_pairs={{0,1},{1,2},{2,3},{3,4},{4,5},{5,6},{6,7},{7,8},{8,9},{9,10},{10,1... | collective-permute-start | bytes 57608 | tf_op jit(solution)/shard_map/ppermute | solution.py:17
  98.2 1.3 collective-permute-start.7
  100.2 3.9 %collective-permute-start.10 = (bf16[3,25,1,128]{3,1,2,0:T(8,128)(2,1)}, bf16[3,25,1,128]{3,1,2,0:T(8,128)(2,1)}, u32[]{:S(2)}, u32[]{:S(2)}) collective-permute-start(bf16[3,25,1,128]{3,1,2,0:T(8,128)(2,1)} %get-tuple-element.83), channel_id=1, source_target_pairs={{0,1},{1,2},{2,3},{3,4},{4,5},{5,6},{6,7},{7,8},{8,9},{9,10},{10,1... | collective-permute-start | bytes 57608 | tf_op jit(solution)/shard_map/ppermute | solution.py:17
  104.1 1.3 collective-permute-start.11
  106.0 1.9 fusion.61
  109.0 1.2 copy.40
  111.2 1.2 copy.41
  113.4 1.2 copy.42
  115.5 1.2 copy.43
  125.2 1.4 convolution_add_fusion.7
  126.6 1.2 convolution_add_fusion.6
  132.3 1.4 convolution_add_fusion.3
  135.9 45.0 %all-reduce.4 = (f32[128]{0:T(128)S(1)}, f32[128]{0:T(128)S(1)}) all-reduce(f32[128]{0:T(128)S(1)} %get-tuple-element.93, f32[128]{0:T(128)S(1)} %get-tuple-element.87), channel_id=1, replica_groups=mesh['ha'=2,'wa'=16] {'ha','wa'}, use_global_device_ids=true, to_apply=%region_2.3 | all-reduce | flops 256 | bytes 2048 | tf_op jit(solution)/shard_map/psum | solution.py:108
  181.9 88.1 %all-reduce.8.cloned.1.call-done = (f32[3,3,3,128,128]{4,3,2,1,0:T(8,128)}, f32[3,3,3,128,128]{4,3,2,1,0:T(8,128)}) async-done(((f32[3,3,3,128,128]{4,3,2,1,0:T(8,128)}, f32[3,3,3,128,128]{4,3,2,1,0:T(8,128)}), (f32[3,3,3,128,128]{4,3,2,1,0:T(8,128)}, f32[3,3,3,128,128]{4,3,2,1,0:T(8,128)})) %all-reduce.8.cloned.1.call-update) | async-done | bytes 3538960 | tf_op jit(solution)/shard_map/psum | solution.py:108
  270.0 3.1 %broadcast_multiply_fusion = f32[3,3,3,128,128]{4,3,2,1,0:T(8,128)} fusion(f32[3,3,3,128,128]{4,3,2,1,0:T(8,128)} %get-tuple-element.8), kind=kLoop, calls=%fused_computation.76 | loop fusion | flops 442368 | bytes 3538944 | tf_op jit(solution)/shard_map/mul | solution.py:111
  273.1 1.4 broadcast_multiply_fusion.1
  (232 shorter events, 52.5 us)
Async XLA Ops:
  7.2 10.5 %copy-start = (bf16[3,3,3,128,128]{4,3,2,1,0:T(8,128)(2,1)S(1)}, bf16[3,3,3,128,128]{4,3,2,1,0:T(8,128)(2,1)}, u32[]{:S(2)}) copy-start(bf16[3,3,3,128,128]{4,3,2,1,0:T(8,128)(2,1)} %param.11) | copy-start | bytes 2654212
  7.2 262.8 %all-reduce.8.cloned.1.call-start = ((), (), s32[]{:S(2)}) async-start(), calls=%async_computation | async-start | bytes 7077888 | tf_op jit(solution)/shard_map/psum | solution.py:108
  9.3 12.9 %collective-permute-start = (bf16[2,3,1,10,128]{4,2,3,1,0:T(2,128)(2,1)S(1)}, bf16[2,3,1,10,128]{4,2,3,1,0:T(2,128)(2,1)S(1)}, u32[]{:S(2)}, u32[]{:S(2)}) collective-permute-start(bf16[2,3,1,10,128]{4,2,3,1,0:T(2,128)(2,1)S(1)} %get-tuple-element.75), channel_id=1, source_target_pairs={{0,16},{1,17},{2,18},{3,19},{4,20},{5,21},{6,22},{7,23},{8,24},{9,... | collective-permute-start | bytes 46088 | tf_op jit(solution)/shard_map/ppermute | solution.py:17
  14.2 8.0 %collective-permute-start.1 = (bf16[2,3,1,10,128]{4,2,3,1,0:T(2,128)(2,1)S(1)}, bf16[2,3,1,10,128]{4,2,3,1,0:T(2,128)(2,1)S(1)}, u32[]{:S(2)}, u32[]{:S(2)}) collective-permute-start(bf16[2,3,1,10,128]{4,2,3,1,0:T(2,128)(2,1)S(1)} %get-tuple-element.76), channel_id=1, source_target_pairs={{16,0},{17,1},{18,2},{19,3},{20,4},{21,5},{22,6},{23,7},{24,8},{25... | collective-permute-start | bytes 46088 | tf_op jit(solution)/shard_map/ppermute | solution.py:19
  22.3 3.7 %collective-permute-start.2 = (bf16[2,3,25,1,128]{4,2,3,1,0:T(8,128)(2,1)S(1)}, bf16[2,3,25,1,128]{4,2,3,1,0:T(8,128)(2,1)S(1)}, u32[]{:S(2)}, u32[]{:S(2)}) collective-permute-start(bf16[2,3,25,1,128]{4,2,3,1,0:T(8,128)(2,1)S(1)} %get-tuple-element.73), channel_id=1, source_target_pairs={{0,1},{1,2},{2,3},{3,4},{4,5},{5,6},{6,7},{7,8},{8,9},{9,10},{10,1... | collective-permute-start | bytes 115208 | tf_op jit(solution)/shard_map/ppermute | solution.py:17
  23.7 4.7 %collective-permute-start.3 = (bf16[2,3,25,1,128]{4,2,3,1,0:T(8,128)(2,1)S(1)}, bf16[2,3,25,1,128]{4,2,3,1,0:T(8,128)(2,1)S(1)}, u32[]{:S(2)}, u32[]{:S(2)}) collective-permute-start(bf16[2,3,25,1,128]{4,2,3,1,0:T(8,128)(2,1)S(1)} %get-tuple-element.74), channel_id=1, source_target_pairs={{1,0},{2,1},{3,2},{4,3},{5,4},{6,5},{7,6},{8,7},{9,8},{10,9},{11,1... | collective-permute-start | bytes 115208 | tf_op jit(solution)/shard_map/ppermute | solution.py:19
  43.2 2.1 copy-start.29
  66.6 2.4 copy-start.16
  67.6 2.7 copy-start.17
  67.6 2.7 copy-start.50
  67.6 3.1 %copy-start.18 = (bf16[690,384]{1,0:T(8,128)(2,1)S(1)}, bf16[690,384]{1,0:T(8,128)(2,1)}, u32[]{:S(2)}) copy-start(bf16[690,384]{1,0:T(8,128)(2,1)} %reshape.144) | copy-start | bytes 1589764
  67.6 3.1 %copy-start.49 = (bf16[1,1,3,128,128]{4,3,2,1,0:T(8,128)(2,1)S(1)}, bf16[1,1,3,128,128]{4,3,2,1,0:T(8,128)(2,1)}, u32[]{:S(2)}) copy-start(bf16[1,1,3,128,128]{4,3,2,1,0:T(8,128)(2,1)} %get-tuple-element.50) | copy-start | bytes 294916
  68.9 2.1 copy-start.19
  69.0 2.1 copy-start.48
  72.6 2.1 copy-start.3
  73.0 3.1 %copy-start.4 = (bf16[690,384]{1,0:T(8,128)(2,1)S(1)}, bf16[690,384]{1,0:T(8,128)(2,1)}, u32[]{:S(2)}) copy-start(bf16[690,384]{1,0:T(8,128)(2,1)} %reshape.133) | copy-start | bytes 1589764
  73.0 3.1 %copy-start.43 = (bf16[1,1,3,128,128]{4,3,2,1,0:T(8,128)(2,1)S(1)}, bf16[1,1,3,128,128]{4,3,2,1,0:T(8,128)(2,1)}, u32[]{:S(2)}) copy-start(bf16[1,1,3,128,128]{4,3,2,1,0:T(8,128)(2,1)} %get-tuple-element.60) | copy-start | bytes 294916
  73.3 3.2 %copy-start.5 = (bf16[690,384]{1,0:T(8,128)(2,1)S(1)}, bf16[690,384]{1,0:T(8,128)(2,1)}, u32[]{:S(2)}) copy-start(bf16[690,384]{1,0:T(8,128)(2,1)} %reshape.134) | copy-start | bytes 1589764
  73.3 3.2 %copy-start.42 = (bf16[1,1,3,128,128]{4,3,2,1,0:T(8,128)(2,1)S(1)}, bf16[1,1,3,128,128]{4,3,2,1,0:T(8,128)(2,1)}, u32[]{:S(2)}) copy-start(bf16[1,1,3,128,128]{4,3,2,1,0:T(8,128)(2,1)} %get-tuple-element.59) | copy-start | bytes 294916
  74.6 2.3 copy-start.6
  74.6 2.3 copy-start.41
  76.5 1.2 copy-start.8
  76.5 1.2 copy-start.39
  76.9 1.2 copy-start.9
  76.9 1.2 copy-start.38
  79.6 14.7 %collective-permute-start.4 = (bf16[3,1,10,128]{3,1,2,0:T(2,128)(2,1)S(1)}, bf16[3,1,10,128]{3,1,2,0:T(2,128)(2,1)S(1)}, u32[]{:S(2)}, u32[]{:S(2)}) collective-permute-start(bf16[3,1,10,128]{3,1,2,0:T(2,128)(2,1)S(1)} %get-tuple-element.91), channel_id=1, source_target_pairs={{0,16},{1,17},{2,18},{3,19},{4,20},{5,21},{6,22},{7,23},{8,24},{9,... | collective-permute-start | bytes 23048 | tf_op jit(solution)/shard_map/ppermute | solution.py:17
  84.1 10.1 %collective-permute-start.5 = (bf16[3,1,10,128]{3,1,2,0:T(2,128)(2,1)S(1)}, bf16[3,1,10,128]{3,1,2,0:T(2,128)(2,1)S(1)}, u32[]{:S(2)}, u32[]{:S(2)}) collective-permute-start(bf16[3,1,10,128]{3,1,2,0:T(2,128)(2,1)S(1)} %get-tuple-element.92), channel_id=1, source_target_pairs={{16,0},{17,1},{18,2},{19,3},{20,4},{21,5},{22,6},{23,7},{24,8},{25... | collective-permute-start | bytes 23048 | tf_op jit(solution)/shard_map/ppermute | solution.py:19
  85.5 14.0 %collective-permute-start.8 = (bf16[3,1,10,128]{3,1,2,0:T(2,128)(2,1)S(1)}, bf16[3,1,10,128]{3,1,2,0:T(2,128)(2,1)S(1)}, u32[]{:S(2)}, u32[]{:S(2)}) collective-permute-start(bf16[3,1,10,128]{3,1,2,0:T(2,128)(2,1)S(1)} %get-tuple-element.89), channel_id=1, source_target_pairs={{0,16},{1,17},{2,18},{3,19},{4,20},{5,21},{6,22},{7,23},{8,24},{9,... | collective-permute-start | bytes 23048 | tf_op jit(solution)/shard_map/ppermute | solution.py:17
  90.0 9.5 %collective-permute-start.9 = (bf16[3,1,10,128]{3,1,2,0:T(2,128)(2,1)S(1)}, bf16[3,1,10,128]{3,1,2,0:T(2,128)(2,1)S(1)}, u32[]{:S(2)}, u32[]{:S(2)}) collective-permute-start(bf16[3,1,10,128]{3,1,2,0:T(2,128)(2,1)S(1)} %get-tuple-element.90), channel_id=1, source_target_pairs={{16,0},{17,1},{18,2},{19,3},{20,4},{21,5},{22,6},{23,7},{24,8},{25... | collective-permute-start | bytes 23048 | tf_op jit(solution)/shard_map/ppermute | solution.py:19
  94.3 11.1 %copy-start.27 = (f32[9,384,128]{2,1,0:T(8,128)}, f32[9,384,128]{2,1,0:T(8,128)S(1)}, u32[]{:S(2)}) copy-start(f32[9,384,128]{2,1,0:T(8,128)S(1)} %fusion.9) | copy-start | bytes 5308420
  94.3 11.1 %collective-permute-start.6 = (bf16[3,25,1,128]{3,1,2,0:T(8,128)(2,1)S(1)}, bf16[3,25,1,128]{3,1,2,0:T(8,128)(2,1)S(1)}, u32[]{:S(2)}, u32[]{:S(2)}) collective-permute-start(bf16[3,25,1,128]{3,1,2,0:T(8,128)(2,1)S(1)} %get-tuple-element.85), channel_id=1, source_target_pairs={{0,1},{1,2},{2,3},{3,4},{4,5},{5,6},{6,7},{7,8},{8,9},{9,10},{10,1... | collective-permute-start | bytes 57608 | tf_op jit(solution)/shard_map/ppermute | solution.py:17
  98.2 7.2 %collective-permute-start.7 = (bf16[3,25,1,128]{3,1,2,0:T(8,128)(2,1)S(1)}, bf16[3,25,1,128]{3,1,2,0:T(8,128)(2,1)S(1)}, u32[]{:S(2)}, u32[]{:S(2)}) collective-permute-start(bf16[3,25,1,128]{3,1,2,0:T(8,128)(2,1)S(1)} %get-tuple-element.86), channel_id=1, source_target_pairs={{1,0},{2,1},{3,2},{4,3},{5,4},{6,5},{7,6},{8,7},{9,8},{10,9},{11,1... | collective-permute-start | bytes 57608 | tf_op jit(solution)/shard_map/ppermute | solution.py:19
  99.5 6.5 %copy-start.52 = (bf16[3,1,10,128]{3,1,2,0:T(2,128)(2,1)}, bf16[3,1,10,128]{3,1,2,0:T(2,128)(2,1)S(1)}, u32[]{:S(2)}) copy-start(bf16[3,1,10,128]{3,1,2,0:T(2,128)(2,1)S(1)} %collective-permute-done.9) | copy-start | bytes 23044
  100.2 17.5 %collective-permute-start.10 = (bf16[3,25,1,128]{3,1,2,0:T(8,128)(2,1)}, bf16[3,25,1,128]{3,1,2,0:T(8,128)(2,1)}, u32[]{:S(2)}, u32[]{:S(2)}) collective-permute-start(bf16[3,25,1,128]{3,1,2,0:T(8,128)(2,1)} %get-tuple-element.83), channel_id=1, source_target_pairs={{0,1},{1,2},{2,3},{3,4},{4,5},{5,6},{6,7},{7,8},{8,9},{9,10},{10,1... | collective-permute-start | bytes 57608 | tf_op jit(solution)/shard_map/ppermute | solution.py:17
  104.1 13.6 %collective-permute-start.11 = (bf16[3,25,1,128]{3,1,2,0:T(8,128)(2,1)}, bf16[3,25,1,128]{3,1,2,0:T(8,128)(2,1)}, u32[]{:S(2)}, u32[]{:S(2)}) collective-permute-start(bf16[3,25,1,128]{3,1,2,0:T(8,128)(2,1)} %get-tuple-element.84), channel_id=1, source_target_pairs={{1,0},{2,1},{3,2},{4,3},{5,4},{6,5},{7,6},{8,7},{9,8},{10,9},{11,1... | collective-permute-start | bytes 57608 | tf_op jit(solution)/shard_map/ppermute | solution.py:19
  122.3 1.8 copy-start.28
  124.1 2.5 copy-start.11
  124.1 3.7 %copy-start.12 = (bf16[690,384]{1,0:T(8,128)(2,1)S(1)}, bf16[690,384]{1,0:T(8,128)(2,1)}, u32[]{:S(2)}) copy-start(bf16[690,384]{1,0:T(8,128)(2,1)} %reshape.154) | copy-start | bytes 1589764
  124.1 3.7 %copy-start.37 = (bf16[1,1,3,128,128]{4,3,2,1,0:T(8,128)(2,1)S(1)}, bf16[1,1,3,128,128]{4,3,2,1,0:T(8,128)(2,1)}, u32[]{:S(2)}) copy-start(bf16[1,1,3,128,128]{4,3,2,1,0:T(8,128)(2,1)} %get-tuple-element.41) | copy-start | bytes 294916
  125.1 3.1 %copy-start.13 = (bf16[690,384]{1,0:T(8,128)(2,1)S(1)}, bf16[690,384]{1,0:T(8,128)(2,1)}, u32[]{:S(2)}) copy-start(bf16[690,384]{1,0:T(8,128)(2,1)} %reshape.155) | copy-start | bytes 1589764
  125.2 3.1 %copy-start.36 = (bf16[1,1,3,128,128]{4,3,2,1,0:T(8,128)(2,1)S(1)}, bf16[1,1,3,128,128]{4,3,2,1,0:T(8,128)(2,1)}, u32[]{:S(2)}) copy-start(bf16[1,1,3,128,128]{4,3,2,1,0:T(8,128)(2,1)} %get-tuple-element.40) | copy-start | bytes 294916
  130.9 1.3 copy-start.24
  130.9 1.3 copy-start.35
  131.9 1.7 copy-start.34
  132.1 2.0 copy-start.25
  132.1 2.0 copy-start.33
  132.3 2.1 copy-start.32
  270.0 3.1 %copy-start.26 = (f32[3,3,3,128,128]{4,3,2,1,0:T(8,128)S(1)}, f32[3,3,3,128,128]{4,3,2,1,0:T(8,128)}, u32[]{:S(2)}) copy-start(f32[3,3,3,128,128]{4,3,2,1,0:T(8,128)} %get-tuple-element.7) | copy-start | bytes 5308420
  (23 other events, 25.2 us)
Sparse Core Ops, SparseCore 0:
  124.3 145.6 all-reduce.7
where the time goes:
time: 283 us; the launch traced here: 281 us
  waiting for transfers between devices  90.6 us (32%)
  local copies, waits for them, and re-layouts  62.4 us (22%)
  blocking collectives  45 us (16%)
  starting transfers between devices  31 us (11%)
  matrix products  24.2 us (9%)
  between operations  15.4 us (5%)
  other arithmetic  12.8 us (5%)
    psum x1, waiting for transfers between devices, body(): lax.psum((grad_one, bias_a, grad_two, bias_b), ('ha', 'wa'))  88.1 us
    psum x1, blocking collectives, body(): lax.psum((grad_one, bias_a, grad_two, bias_b), ('ha', 'wa'))  45 us
    reshape x27, local copies, waits for them, and re-layouts, convolve(): wide[step_t:step_t + frames, step_h:step_h + rows].reshape(-1, 3 * inner)  25.2 us
    slice x30, local copies, waits for them, and re-layouts, convolve(): wide[step_t:step_t + frames, step_h:step_h + rows].reshape(-1, 3 * inner)  25.2 us
    ppermute x6, starting transfers between devices, with_halo(): lax.ppermute(tail, axis, [(i, (i + 1) % count) for i in range(ends)])  23.3 us
    dot_general x27, matrix products, convolve(): jnp.dot(slab, kernel[step_t, step_h].reshape(3 * inner, -1), preferred_el...  17.8 us
    ppermute x6, starting transfers between devices, with_halo(): lax.ppermute(head, axis, [((i + 1) % count, i) for i in range(ends)])  7.74 us
    dot_general x18, matrix products, kernel_terms(): lax.dot_general(slab, grads, (((0,), (0,)), ((), ())), preferred_element_...  6.47 us
  transfers between devices with their start and end apart: 13, of which 2 were waited for; matrix products, arithmetic and copies ran while one was open for 12% of the time, Pallas kernels for 0%

commit v1 on v0

v1 whole, which is shorter than its diff:
```python
import functools
import math

import jax
import jax.numpy as jnp
from jax import lax
from jax.experimental import pallas as pl
from jax.experimental.pallas import tpu as pltpu
from jax.sharding import PartitionSpec as P

MESH = pl.DeviceIdType.MESH
F32 = jnp.float32
BF16 = jnp.bfloat16
VMEM = pl.BlockSpec(memory_space=pltpu.VMEM)
DIRECTIONS = [(dy, dx) for dy in (-1, 0, 1) for dx in (-1, 0, 1) if (dy, dx) != (0, 0)]
RIM = 2


def span(step, size):
    return {-1: (0, RIM), 0: (0, size), 1: (size - RIM, size)}[step]


def rim_shape(direction, frames, rows, columns, chans):
    dy, dx = direction
    return (2 * frames, rows if dy == 0 else RIM, columns if dx == 0 else RIM, chans)


def neighbour(direction, me, sizes):
    there = [m + d for m, d in zip(me, direction)]
    exists = True
    for place, size, d in zip(there, sizes, direction):
        if d < 0:
            exists = jnp.logical_and(exists, place >= 0)
        if d > 0:
            exists = jnp.logical_and(exists, place < size)
    return exists, tuple(there)


def halo_kernel(sizes, x_ref, g_ref, *refs):
    recv = refs[:8]
    stage = refs[8:16]
    send_sem, recv_sem = refs[16:]
    frames, rows, columns, _ = x_ref.shape
    me = (lax.axis_index("ha"), lax.axis_index("wa"))
    barrier = pltpu.get_barrier_semaphore()
    places = [neighbour(d, me, sizes) for d in DIRECTIONS]
    for exists, there in places:

        @pl.when(exists)
        def _(there=there):
            pl.semaphore_signal(barrier, inc=1, device_id=there, device_id_type=MESH)

    for which, ref in enumerate((x_ref, g_ref)):
        whole = ref[...].astype(F32)
        for k, (dy, dx) in enumerate(DIRECTIONS):
            r0, r1 = span(dy, rows)
            c0, c1 = span(dx, columns)
            stage[k][which * frames : (which + 1) * frames] = whole[:, r0:r1, c0:c1].astype(BF16)
    pl.semaphore_wait(barrier, sum(jnp.where(exists, 1, 0) for exists, _ in places))
    copies = []
    for k, (exists, there) in enumerate(places):
        opposite = 7 - k
        copy = pltpu.make_async_remote_copy(
            src_ref=stage[k],
            dst_ref=recv[opposite],
            send_sem=send_sem.at[k],
            recv_sem=recv_sem.at[opposite],
            device_id=there,
            device_id_type=MESH,
        )
        pl.when(exists)(copy.start)
        copies.append(copy)
    for k, (exists, there) in enumerate(places):

        @pl.when(exists)
        def _(k=k, there=there):
            copies[k].wait_send()
            pltpu.make_async_remote_copy(
                src_ref=stage[k],
                dst_ref=recv[k],
                send_sem=send_sem.at[k],
                recv_sem=recv_sem.at[k],
                device_id=there,
                device_id_type=MESH,
            ).wait_recv()


def halo(x, g, sizes):
    frames, rows, columns, chans = x.shape
    shapes = [rim_shape(d, frames, rows, columns, chans) for d in DIRECTIONS]
    return pl.pallas_call(
        functools.partial(halo_kernel, sizes),
        name="halo",
        out_shape=[jax.ShapeDtypeStruct(s, BF16) for s in shapes],
        in_specs=[VMEM, VMEM],
        out_specs=[VMEM] * 8,
        scratch_shapes=[pltpu.VMEM(s, BF16) for s in shapes]
        + [pltpu.SemaphoreType.DMA((8,)), pltpu.SemaphoreType.DMA((8,))],
        compiler_params=pltpu.CompilerParams(collective_id=0, has_side_effects=True),
    )(x, g)


def sigmoid(value):
    return 1.0 / (1.0 + jnp.exp(-value))


def store_wide(wide, t, value):
    rows, cols, chans = value.shape
    flat = value.reshape(rows * cols, chans)
    for kw in range(3):
        moved = flat if kw == 0 else pltpu.roll(flat, rows * cols - kw, 0)
        wide[t, :, :, kw * chans : (kw + 1) * chans] = moved.reshape(rows, cols, chans).astype(BF16)


def flat2(value):
    return value.reshape(-1, value.shape[-1])


def dot(a, b, dims):
    return lax.dot_general(a, b, (dims, ((), ())), preferred_element_type=F32)


def compute_kernel(
    sizes,
    x_ref,
    g_ref,
    k1_ref,
    b1_ref,
    k2_ref,
    s1_ref,
    h1_ref,
    s2_ref,
    h2_ref,
    *refs,
):
    recv = refs[:8]
    out_ref, terms = refs[8:10]
    pad, w1, wg, w2, wd, ds2, own = refs[10:]
    frames, rows, columns, chans = x_ref.shape
    deep, cols = pad.shape[2:4]
    inner = rows + 2
    taps = 27 * chans
    me = (lax.axis_index("ha"), lax.axis_index("wa"))

    pad[...] = jnp.zeros_like(pad)
    pad[0, :, RIM : RIM + rows, RIM : RIM + columns] = x_ref[...].astype(F32)
    pad[1, :, RIM : RIM + rows, RIM : RIM + columns] = g_ref[...].astype(F32)
    starts = {-1: 0, 0: RIM}
    for k, direction in enumerate(DIRECTIONS):
        exists, _ = neighbour(direction, me, sizes)
        r0 = starts.get(direction[0], RIM + rows)
        c0 = starts.get(direction[1], RIM + columns)
        _, nr, nc, _ = recv[k].shape

        @pl.when(exists)
        def _(k=k, r0=r0, c0=c0, nr=nr, nc=nc):
            value = recv[k][...].astype(F32)
            for which in range(2):
                pad[which, :, r0 : r0 + nr, c0 : c0 + nc] = value[
                    which * frames : (which + 1) * frames
                ]

    def inside(depth, wide, rim):
        shape = (depth, cols, chans)
        r = lax.broadcasted_iota(jnp.int32, shape, 0) + (me[0] * rows - rim)
        c = lax.broadcasted_iota(jnp.int32, shape, 1)
        place = c + (me[1] * columns - rim)
        ok = (r >= 0) & (r < rows * sizes[0]) & (place >= 0) & (place < columns * sizes[1])
        return ok & (c < wide)

    s1 = s1_ref[...]
    h1 = h1_ref[...]
    s2 = s2_ref[...]
    h2 = h2_ref[...]
    ok1 = inside(deep, columns + 2 * RIM, RIM)
    for t in range(frames):
        z1 = pad[0, t] * s1 + h1
        store_wide(w1, t, jnp.where(ok1, z1 * sigmoid(z1), 0.0))
        store_wide(wg, t, pad[1, t])
        own[0, t] = jnp.zeros_like(own[0, t])
        own[0, t, :, :columns] = g_ref[t].astype(F32)

    ok2 = inside(inner, columns + 2, 1)
    for t in range(frames):
        total = jnp.zeros((inner * cols, chans), F32)
        for kt in range(2 - t, 3) if t < 2 else range(3):
            for kh in range(3):
                total = total + dot(
                    flat2(w1[t + kt - 2, kh : kh + inner]),
                    k1_ref[kt, kh].reshape(3 * chans, chans),
                    ((1,), (0,)),
                )
        z2 = (total.reshape(inner, cols, chans) + b1_ref[...]) * s2 + h2
        sig = sigmoid(z2)
        store_wide(w2, t, jnp.where(ok2, z2 * sig, 0.0))
        ds2[t] = jnp.where(ok2, sig * (1.0 + z2 * (1.0 - sig)) * s2, 0.0)

    gown = own[0].astype(BF16)
    for kt in range(3):
        for kh in range(3):
            first = 2 - kt
            slab = w2[: frames - first, kh : kh + rows]
            term = dot(flat2(slab), flat2(gown[first:]), ((0,), (0,)))
            terms[0, (kt * 3 + kh) * 3 * chans : (kt * 3 + kh + 1) * 3 * chans] = term

    def back(wide, kernel_ref, t, depth):
        total = jnp.zeros((depth * cols, chans), F32)
        for kt in range(t, 3):
            for kh in range(3):
                weights = jnp.concatenate(
                    [kernel_ref[kt, 2 - kh, 2 - kw] for kw in range(3)], axis=1
                )
                total = total + dot(
                    flat2(wide[t + 2 - kt, kh : kh + depth]), weights, ((1,), (1,))
                )
        return total.reshape(depth, cols, chans)

    c = lax.broadcasted_iota(jnp.int32, (rows, cols, chans), 1)
    mine = (c >= 1) & (c <= columns)
    bias = [jnp.zeros((1, chans), F32), jnp.zeros((1, chans), F32)]
    for t in range(frames):
        dc1 = (back(wg, k2_ref, t, inner) * ds2[t]).astype(BF16).astype(F32)
        store_wide(wd, t, dc1)
        kept = jnp.where(mine, dc1[1 : 1 + rows], 0.0)
        own[1, t] = kept
        bias[1] = bias[1] + jnp.sum(flat2(kept), axis=0, keepdims=True)
        bias[0] = bias[0] + jnp.sum(flat2(own[0, t]), axis=0, keepdims=True)

    down = own[1].astype(BF16)
    for kt in range(3):
        for kh in range(3):
            first = 2 - kt
            slab = w1[: frames - first, kh + 1 : kh + 1 + rows]
            term = dot(flat2(slab), flat2(down[first:]), ((0,), (0,)))
            terms[1, (kt * 3 + kh) * 3 * chans : (kt * 3 + kh + 1) * 3 * chans] = term
    tail = terms.shape[1] - taps
    for which in range(2):
        lead = lax.broadcasted_iota(jnp.int32, (tail, chans), 0) == 0
        terms[which, taps:] = jnp.where(lead, bias[which], 0.0)

    for t in range(frames):
        da1 = back(wd, k1_ref, t, rows)[:, :columns]
        z1 = x_ref[t].astype(F32) * s1 + h1
        sig = sigmoid(z1)
        slope = sig * (1.0 + z1 * (1.0 - sig))
        out_ref[t] = (g_ref[t].astype(F32) + da1 * slope * s1).astype(BF16)


def round_up(value, step):
    return -(-value // step) * step


def compute(x, g, k1, b1, k2, s1, h1, s2, h2, recv, sizes, height):
    frames, rows, columns, chans = x.shape
    cols = round_up(columns + 2 * RIM, 16)
    deep = rows + 2 * RIM
    vectors = [v.reshape(1, chans) for v in (b1, s1, h1, s2, h2)]
    return pl.pallas_call(
        functools.partial(compute_kernel, sizes),
        name="compute",
        out_shape=[
            jax.ShapeDtypeStruct(x.shape, BF16),
            jax.ShapeDtypeStruct((2, height, chans), F32),
        ],
        in_specs=[VMEM] * 17,
        out_specs=[VMEM] * 2,
        scratch_shapes=[
            pltpu.VMEM((2, frames, deep, cols, chans), F32),
            pltpu.VMEM((frames, deep, cols, 3 * chans), BF16),
            pltpu.VMEM((frames, deep, cols, 3 * chans), BF16),
            pltpu.VMEM((frames, rows + 2, cols, 3 * chans), BF16),
            pltpu.VMEM((frames, rows + 2, cols, 3 * chans), BF16),
            pltpu.VMEM((frames, rows + 2, cols, chans), F32),
            pltpu.VMEM((2, frames, rows, cols, chans), F32),
        ],
    )(x, g, k1, vectors[0], k2, *vectors[1:], *recv)


def reduce_kernel(sizes, factor, taps, in_ref, *refs):
    outs = refs[:4]
    half_send, half_recv, part_send, part_recv, piece_send, piece_recv, summed, full = refs[4:12]
    sems = refs[12:]
    ha, wa = lax.axis_index("ha"), lax.axis_index("wa")
    core, mid, outer = lax.rem(wa, 2), lax.rem(wa // 2, 2), wa // 4
    many_b, many_c = 2 * sizes[0], sizes[1] // 4
    b = ha * 2 + mid
    height = in_ref.shape[1]
    half = height // 2
    part = half // many_b
    piece = part // many_c

    def in_b(j):
        q = lax.rem(b + j, many_b)
        return q, (q // 2, outer * 4 + lax.rem(q, 2) * 2 + core)

    def in_c(j):
        q = lax.rem(outer + j, many_c)
        return q, (ha, q * 4 + mid * 2 + core)

    partner = (ha, wa + 1 - 2 * core)
    barrier = pltpu.get_barrier_semaphore()
    peers = [partner] + [in_b(j)[1] for j in range(1, many_b)]
    peers += [in_c(j)[1] for j in range(1, many_c)]
    for there in peers:
        pl.semaphore_signal(barrier, inc=1, device_id=there, device_id_type=MESH)

    def rows_at(start, size):
        return pl.ds(pl.multiple_of(start, 16), size)

    def send(src, dst, stage, which, slot, there):
        copy = pltpu.make_async_remote_copy(
            src_ref=src,
            dst_ref=dst,
            send_sem=sems[2 * stage].at[which, slot],
            recv_sem=sems[2 * stage + 1].at[which, slot],
            device_id=there,
            device_id_type=MESH,
        )
        copy.start()
        return copy

    copies = {}
    for w in range(2):
        half_send[w] = in_ref[w, rows_at((1 - core) * half, half)].astype(BF16)
        if w == 0:
            pl.semaphore_wait(barrier, len(peers))
        copies["a", w] = [send(half_send.at[w], half_recv.at[w], 0, w, 0, partner)]
    for w in range(2):
        copies["a", w][0].wait_recv()
        total = in_ref[w, rows_at(core * half, half)] + half_recv[w].astype(F32)
        summed[w] = total
        part_send[w] = total.astype(BF16)
        copies["b", w] = []
        for j in range(1, many_b):
            q, there = in_b(j)
            copies["b", w].append(
                send(
                    part_send.at[w, rows_at(q * part, part)],
                    part_recv.at[w, j - 1],
                    1,
                    w,
                    j - 1,
                    there,
                )
            )
    for w in range(2):
        total = summed[w, rows_at(b * part, part)]
        for j in range(1, many_b):
            copies["b", w][j - 1].wait_recv()
            total = total + part_recv[w, j - 1].astype(F32)
        summed[w, :part] = total
        piece_send[w] = total.astype(BF16)
        copies["c", w] = []
        for j in range(1, many_c):
            q, there = in_c(j)
            copies["c", w].append(
                send(
                    piece_send.at[w, rows_at(q * piece, piece)],
                    piece_recv.at[w, j - 1],
                    2,
                    w,
                    j - 1,
                    there,
                )
            )
    part_at = core * half + b * part
    for w in range(2):
        total = summed[w, rows_at(outer * piece, piece)]
        for j in range(1, many_c):
            copies["c", w][j - 1].wait_recv()
            total = total + piece_recv[w, j - 1].astype(F32)
        here = rows_at(part_at + outer * piece, piece)
        full[w, here] = (total * factor).astype(BF16)
        copies["d", w] = [
            send(full.at[w, here], full.at[w, here], 3, w, j - 1, in_c(j)[1])
            for j in range(1, many_c)
        ]
    for w in range(2):
        for copy in copies["d", w]:
            copy.wait_recv()
        here = rows_at(part_at, part)
        copies["e", w] = [
            send(full.at[w, here], full.at[w, here], 4, w, j - 1, in_b(j)[1])
            for j in range(1, many_b)
        ]
    for w in range(2):
        for copy in copies["e", w]:
            copy.wait_recv()
        here = rows_at(core * half, half)
        copies["f", w] = [send(full.at[w, here], full.at[w, here], 5, w, 0, partner)]
    for w in range(2):
        copies["f", w][0].wait_recv()
        outs[w][...] = full[w, :taps].astype(F32)
        outs[2 + w][...] = full[w, taps : taps + 16].astype(F32)[:1]
    for group in copies.values():
        for copy in group:
            copy.wait_send()


def all_reduce(terms, sizes, factor, taps):
    _, height, chans = terms.shape
    many_b, many_c = 2 * sizes[0], sizes[1] // 4
    half = height // 2
    part = half // many_b
    piece = part // many_c
    slots = [1, many_b - 1, many_c - 1, many_c - 1, many_b - 1, 1]
    return pl.pallas_call(
        functools.partial(reduce_kernel, sizes, factor, taps),
        name="reduce",
        out_shape=[jax.ShapeDtypeStruct((taps, chans), F32)] * 2
        + [jax.ShapeDtypeStruct((1, chans), F32)] * 2,
        in_specs=[VMEM],
        out_specs=[VMEM] * 4,
        scratch_shapes=[
            pltpu.VMEM((2, half, chans), BF16),
            pltpu.VMEM((2, half, chans), BF16),
            pltpu.VMEM((2, half, chans), BF16),
            pltpu.VMEM((2, many_b - 1, part, chans), BF16),
            pltpu.VMEM((2, part, chans), BF16),
            pltpu.VMEM((2, many_c - 1, piece, chans), BF16),
            pltpu.VMEM((2, half, chans), F32),
            pltpu.VMEM((2, height, chans), BF16),
        ]
        + [pltpu.SemaphoreType.DMA((2, n)) for n in slots for _ in range(2)],
        compiler_params=pltpu.CompilerParams(collective_id=1, has_side_effects=True),
    )(terms)


def body(sizes, x, g, k1, b1, k2, s1, h1, s2, h2):
    frames, rows, columns, chans = x.shape
    factor = 1.0 / math.sqrt(frames * rows * sizes[0] * columns * sizes[1])
    taps = 27 * chans
    height = round_up(taps + 16, 16 * sizes[0] * sizes[1])
    recv = halo(x, g, sizes)
    grad_input, terms = compute(x, g, k1, b1, k2, s1, h1, s2, h2, recv, sizes, height)
    grad_two, grad_one, bias_b, bias_a = all_reduce(terms, sizes, factor, taps)
    return (
        grad_input,
        grad_one.reshape(k1.shape),
        bias_a.reshape(chans),
        grad_two.reshape(k2.shape),
        bias_b.reshape(chans),
    )


def solution(mesh):
    sizes = (mesh.shape["ha"], mesh.shape["wa"])
    cells = P(None, "ha", "wa", None)
    return jax.shard_map(
        functools.partial(body, sizes),
        mesh=mesh,
        in_specs=(cells, cells) + (P(),) * 7,
        out_specs=(cells, P(), P(), P(), P()),
        check_vma=False,
    )
```

time: 283 us -> 73.4 us (0.26)
  waiting for transfers between devices: 90.6 us -> 0 us
  Pallas kernels: 0 us -> 62.1 us
  local copies, waits for them, and re-layouts: 62.4 us -> 10.3 us
  blocking collectives: 45 us -> 0 us
  starting transfers between devices: 31 us -> 0 us
  matrix products: 24.2 us -> 0 us
  between operations: 15.4 us -> 0.67 us
  other arithmetic: 12.8 us -> 0 us
    psum x1 -> x0, waiting for transfers between devices: 88.1 us -> none  [body(): lax.psum((grad_one, bias_a, grad_two, bias_b), ('ha', 'wa'))]
    pallas_call x0 -> x3, Pallas kernels: none -> 62.1 us  [the longest x1 42.9 us: all_reduce(): pl.pallas_call(functools.partial(reduce_kernel, sizes, factor, taps), nam...]
    psum x1 -> x0, blocking collectives: 45 us -> none  [body(): lax.psum((grad_one, bias_a, grad_two, bias_b), ('ha', 'wa'))]
    ppermute x12 -> x0, starting transfers between devices: 31 us -> none  [the longest x6 23.3 us: with_halo(): lax.ppermute(tail, axis, [(i, (i + 1) % count) for i in range(ends)])]
    slice x38 -> x0, local copies, waits for them, and re-layouts: 31 us -> none  [the longest x30 25.2 us: convolve(): wide[step_t:step_t + frames, step_h:step_h + rows].reshape(-1, 3 * inner)]
    reshape x30 -> x0, local copies, waits for them, and re-layouts: 25.4 us -> none  [the longest x27 25.2 us: convolve(): wide[step_t:step_t + frames, step_h:step_h + rows].reshape(-1, 3 * inner)]
    dot_general x45 -> x0, matrix products: 24.2 us -> none  [the longest x27 17.8 us: convolve(): jnp.dot(slab, kernel[step_t, step_h].reshape(3 * inner, -1), preferred_el...]
    mul x4 -> x0, other arithmetic: 5.5 us -> none  [the longest x1 3.05 us: body(): grad_two * factor]
  transfers between devices with their start and end apart: 13 -> 0, of which waited for: 2 -> 0; matrix products, arithmetic and copies ran while one was open for 12% -> 0% of each run, Pallas kernels for 0% -> 0%
where the time goes in v1:
time: 73.4 us; the launch traced here: 73.1 us
  Pallas kernels  62.1 us (85%)
  local copies, waits for them, and re-layouts  10.3 us (14%)
    pallas_call x1, Pallas kernels, all_reduce(): pl.pallas_call(functools.partial(reduce_kernel, sizes, factor, taps), nam...  42.9 us
    pallas_call x1, Pallas kernels, compute(): pl.pallas_call(functools.partial(compute_kernel, sizes), name='compute',...  11.8 us
    unnamed x13, local copies, waits for them, and re-layouts  10.3 us
    pallas_call x1, Pallas kernels, halo(): pl.pallas_call(functools.partial(halo_kernel, sizes), name='halo', out_sh...  7.41 us

profile of v1, /device:TPU:0, one launch (start us, length us, event | category | flops | bytes accessed | tf_op | source)
XLA Modules:
  0.0 73.1 jit_solution(3499986681913911969)
XLA Ops:
  0.6 1.7 %copy.16.x_ref = bf16[3,23,10,128]{3,2,1,0:T(8,128)(2,1)} copy(bf16[3,23,10,128]{3,1,2,0:T(8,128)(2,1)} %param.9) | data formatting | bytes 353280 | tf_op args[0]
  2.3 1.7 %copy.17.g_ref = bf16[3,23,10,128]{3,2,1,0:T(8,128)(2,1)} copy(bf16[3,23,10,128]{3,1,2,0:T(8,128)(2,1)} %param.10) | data formatting | bytes 353280 | tf_op args[1]
  4.0 7.4 %halo.1 = (bf16[6,2,2,128]{3,2,1,0:T(2,128)(2,1)}, bf16[6,2,10,128]{3,2,1,0:T(8,128)(2,1)}, bf16[6,2,2,128]{3,2,1,0:T(2,128)(2,1)}, bf16[6,23,2,128]{3,2,1,0:T(2...) custom-call(bf16[3,23,10,128]{3,2,1,0:T(8,128)(2,1)} %copy.16.x_ref,, ...), custom_call_target="tpu_custom_call" | custom-call | tf_op jit(solution)/shard_map/halo/pallas_call | solution.py:91
  11.4 11.8 %compute.1 = (bf16[3,23,10,128]{3,2,1,0:T(8,128)(2,1)}, f32[2,3584,128]{2,1,0:T(8,128)}) custom-call(bf16[3,23,10,128]{3,2,1,0:T(8,128)(2,1)} %copy.16.x_ref, bf16[3,23,10,128]{3,2,1,0:T(8,128)(2,1)} %copy.17.g_ref, bf16[3,3,3,128,128]{4,3,2,1,0:T(8,128)(2,1)} %k1_ref.1, f32[1,128]{1,0:T(1,128)} %bitcast.11, bf16[3,3,3,128,128]{4,3,2,1,0:T(8,128)(2,1)} %k2_ref.1, ...), custom_call_target="tpu_custom_call" | custom-call | tf_op jit(solution)/shard_map/compute/pallas_call | solution.py:258
  23.2 1.7 %copy.18 = bf16[3,23,10,128]{3,1,2,0:T(8,128)(2,1)} copy(bf16[3,23,10,128]{3,2,1,0:T(8,128)(2,1)} %get-tuple-element.33) | data formatting | bytes 353280
  24.9 42.9 %reduce.1 = (f32[3456,128]{1,0:T(8,128)}, f32[3456,128]{1,0:T(8,128)}, f32[1,128]{1,0:T(1,128)}, f32[1,128]{1,0:T(1,128)}) custom-call(f32[2,3584,128]{2,1,0:T(8,128)} %get-tuple-element.28.in_ref), custom_call_target="tpu_custom_call" | custom-call | tf_op jit(solution)/shard_map/reduce/pallas_call | solution.py:407
  67.8 0.0 copy-start.2
  67.8 0.0 copy-start
  67.9 3.0 %copy.23 = f32[3,3,3,128,128]{4,3,2,1,0:T(8,128)} copy(f32[3,3,3,128,128]{4,3,2,1,0:T(8,128)} %bitcast.10) | data formatting | bytes 3538944
  70.9 0.0 copy-done.2
  70.9 0.5 copy.24
  71.4 0.0 copy-done
  71.4 0.0 copy-start.1
  71.4 1.2 %copy.25 = f32[3,3,3,128,128]{4,3,2,1,0:T(8,128)} copy(f32[3,3,3,128,128]{4,3,2,1,0:T(8,128)S(1)} %bitcast.9) | data formatting | bytes 3538944
  72.6 0.0 copy-done.1
  72.6 0.5 copy.26
Async XLA Ops:
  67.8 3.0 %copy-start.2 = (f32[1,128]{1,0:T(1,128)S(1)}, f32[1,128]{1,0:T(1,128)}, u32[]{:S(2)}) copy-start(f32[1,128]{1,0:T(1,128)} %get-tuple-element.30) | copy-start | bytes 1540
  67.8 3.5 %copy-start = (f32[3456,128]{1,0:T(8,128)S(1)}, f32[3456,128]{1,0:T(8,128)}, u32[]{:S(2)}) copy-start(f32[3456,128]{1,0:T(8,128)} %get-tuple-element.31) | copy-start | bytes 5308420
  71.4 1.2 %copy-start.1 = (f32[1,128]{1,0:T(1,128)S(1)}, f32[1,128]{1,0:T(1,128)}, u32[]{:S(2)}) copy-start(f32[1,128]{1,0:T(1,128)} %get-tuple-element.32) | copy-start | bytes 1540

commit v2 on v0

v2 whole, which is shorter than its diff:
```python
import functools
import math

import jax
import jax.numpy as jnp
from jax import lax
from jax.experimental import pallas as pl
from jax.experimental.pallas import tpu as pltpu
from jax.sharding import PartitionSpec as P

MESH = pl.DeviceIdType.MESH
F32 = jnp.float32
BF16 = jnp.bfloat16
VMEM = pl.BlockSpec(memory_space=pltpu.VMEM)
DIRECTIONS = [(dy, dx) for dy in (-1, 0, 1) for dx in (-1, 0, 1) if (dy, dx) != (0, 0)]
RIM = 2


def span(step, size):
    return {-1: (0, RIM), 0: (0, size), 1: (size - RIM, size)}[step]


def rim_shape(direction, frames, rows, columns, chans):
    dy, dx = direction
    return (2 * frames, rows if dy == 0 else RIM, columns if dx == 0 else RIM, chans)


def neighbour(direction, me, sizes):
    there = [m + d for m, d in zip(me, direction)]
    exists = True
    for place, size, d in zip(there, sizes, direction):
        if d < 0:
            exists = jnp.logical_and(exists, place >= 0)
        if d > 0:
            exists = jnp.logical_and(exists, place < size)
    return exists, (there[1], there[0])


def sigmoid(value):
    return 1.0 / (1.0 + jnp.exp(-value))


def store_wide(wide, t, value):
    rows, cols, chans = value.shape
    flat = value.reshape(rows * cols, chans)
    for kw in range(3):
        moved = flat if kw == 0 else pltpu.roll(flat, rows * cols - kw, 0)
        wide[t, :, :, kw * chans : (kw + 1) * chans] = moved.reshape(rows, cols, chans).astype(BF16)


def flat2(value):
    return value.reshape(-1, value.shape[-1])


def dot(a, b, dims):
    return lax.dot_general(a, b, (dims, ((), ())), preferred_element_type=F32)


def round_up(value, step):
    return -(-value // step) * step


def rows_at(start, size):
    return pl.ds(pl.multiple_of(start, 16), size)


class Reducer:
    def __init__(self, sizes, factor, terms, refs, sems, full):
        self.factor, self.terms, self.full, self.sems = factor, terms, full, sems
        (
            self.half_send,
            self.half_recv,
            self.part_send,
            self.part_recv,
            self.piece_send,
            self.piece_recv,
            self.summed,
        ) = refs
        self.ha, self.wa = lax.axis_index("ha"), lax.axis_index("wa")
        self.core = lax.rem(self.wa, 2)
        self.mid = lax.rem(self.wa // 2, 2)
        self.outer = self.wa // 4
        self.many_b, self.many_c = 2 * sizes[0], sizes[1] // 4
        self.b = self.ha * 2 + self.mid
        self.half = terms.shape[1] // 2
        self.part = self.half // self.many_b
        self.piece = self.part // self.many_c
        self.partner = (self.ha, self.wa + 1 - 2 * self.core)
        self.peers = [self.partner]
        self.peers += [self.in_b(j)[1] for j in range(1, self.many_b)]
        self.peers += [self.in_c(j)[1] for j in range(1, self.many_c)]
        self.copies = {}

    def in_b(self, j):
        q = lax.rem(self.b + j, self.many_b)
        return q, (q // 2, self.outer * 4 + lax.rem(q, 2) * 2 + self.core)

    def in_c(self, j):
        q = lax.rem(self.outer + j, self.many_c)
        return q, (self.ha, q * 4 + self.mid * 2 + self.core)

    def send(self, src, dst, stage, which, slot, there):
        copy = pltpu.make_async_remote_copy(
            src_ref=src,
            dst_ref=dst,
            send_sem=self.sems[2 * stage].at[which, slot],
            recv_sem=self.sems[2 * stage + 1].at[which, slot],
            device_id=there,
            device_id_type=MESH,
        )
        copy.start()
        self.copies.setdefault((stage, which), []).append(copy)

    def arrive(self, stage, which):
        for copy in self.copies[stage, which]:
            copy.wait_recv()

    def start(self, w):
        half = self.half
        self.half_send[w] = self.terms[w, rows_at((1 - self.core) * half, half)].astype(BF16)
        self.send(self.half_send.at[w], self.half_recv.at[w], 0, w, 0, self.partner)

    def halves(self, w):
        self.arrive(0, w)
        total = self.terms[w, rows_at(self.core * self.half, self.half)]
        total = total + self.half_recv[w].astype(F32)
        self.summed[w] = total
        self.part_send[w] = total.astype(BF16)
        for j in range(1, self.many_b):
            q, there = self.in_b(j)
            src = self.part_send.at[w, rows_at(q * self.part, self.part)]
            self.send(src, self.part_recv.at[w, j - 1], 1, w, j - 1, there)

    def parts(self, w):
        total = self.summed[w, rows_at(self.b * self.part, self.part)]
        self.arrive(1, w)
        for j in range(1, self.many_b):
            total = total + self.part_recv[w, j - 1].astype(F32)
        self.summed[w, : self.part] = total
        self.piece_send[w] = total.astype(BF16)
        for j in range(1, self.many_c):
            q, there = self.in_c(j)
            src = self.piece_send.at[w, rows_at(q * self.piece, self.piece)]
            self.send(src, self.piece_recv.at[w, j - 1], 2, w, j - 1, there)

    def pieces(self, w):
        total = self.summed[w, rows_at(self.outer * self.piece, self.piece)]
        self.arrive(2, w)
        for j in range(1, self.many_c):
            total = total + self.piece_recv[w, j - 1].astype(F32)
        start = self.core * self.half + self.b * self.part + self.outer * self.piece
        here = rows_at(start, self.piece)
        self.full[w, here] = (total * self.factor).astype(BF16)
        for j in range(1, self.many_c):
            self.spread(w, here, 3, j, self.in_c(j)[1])

    def spread(self, w, here, stage, j, there):
        self.send(self.full.at[w, here], self.full.at[w, here], stage, w, j - 1, there)

    def join_pieces(self, w):
        self.arrive(3, w)
        here = rows_at(self.core * self.half + self.b * self.part, self.part)
        for j in range(1, self.many_b):
            self.spread(w, here, 4, j, self.in_b(j)[1])

    def join_parts(self, w):
        self.arrive(4, w)
        here = rows_at(self.core * self.half, self.half)
        self.spread(w, here, 5, 1, self.partner)

    def finish(self, w):
        self.arrive(5, w)
        for stage in range(6):
            for copy in self.copies[stage, w]:
                copy.wait_send()


def block_kernel(
    sizes,
    factor,
    x_ref,
    g_ref,
    k1_hbm,
    b1_ref,
    k2_hbm,
    s1_ref,
    h1_ref,
    s2_ref,
    h2_ref,
    out_ref,
    full,
    *refs,
):
    recv, stage = refs[:8], refs[8:16]
    send_sem, recv_sem, load_sem, k1_ref, k2_ref = refs[16:21]
    pad, w1, wg, w2, wd, ds2, own, terms = refs[21:29]
    reducer = Reducer(sizes, factor, terms, refs[29:36], refs[36:], full)
    frames, rows, columns, chans = x_ref.shape
    deep, cols = pad.shape[2:4]
    inner = rows + 2
    taps = 27 * chans
    grid = (sizes[1], sizes[0])
    me = (lax.axis_index("wa"), lax.axis_index("ha"))
    loads = [
        pltpu.make_async_copy(k1_hbm, k1_ref, load_sem.at[0]),
        pltpu.make_async_copy(k2_hbm, k2_ref, load_sem.at[1]),
    ]
    for load in loads:
        load.start()

    barrier = pltpu.get_barrier_semaphore()
    places = [neighbour(d, me, grid) for d in DIRECTIONS]
    for exists, there in places:

        @pl.when(exists)
        def _(there=there):
            pl.semaphore_signal(barrier, inc=1, device_id=there, device_id_type=MESH)

    for there in reducer.peers:
        pl.semaphore_signal(barrier, inc=1, device_id=there, device_id_type=MESH)
    for which, ref in enumerate((x_ref, g_ref)):
        whole = ref[...].astype(F32)
        for k, (dr, dc) in enumerate(DIRECTIONS):
            r0, r1 = span(dr, rows)
            c0, c1 = span(dc, columns)
            stage[k][which * frames : (which + 1) * frames] = whole[:, r0:r1, c0:c1].astype(BF16)
    count = sum(jnp.where(exists, 1, 0) for exists, _ in places)
    pl.semaphore_wait(barrier, count + len(reducer.peers))
    copies = []
    for k, (exists, there) in enumerate(places):
        copy = pltpu.make_async_remote_copy(
            src_ref=stage[k],
            dst_ref=recv[7 - k],
            send_sem=send_sem.at[k],
            recv_sem=recv_sem.at[7 - k],
            device_id=there,
            device_id_type=MESH,
        )
        pl.when(exists)(copy.start)
        copies.append(copy)

    pad[...] = jnp.zeros_like(pad)
    pad[0, :, RIM : RIM + rows, RIM : RIM + columns] = x_ref[...].astype(F32)
    pad[1, :, RIM : RIM + rows, RIM : RIM + columns] = g_ref[...].astype(F32)
    for t in range(frames):
        own[0, t] = jnp.zeros_like(own[0, t])
        own[0, t, :, :columns] = g_ref[t].astype(F32)

    starts = {-1: 0, 0: RIM}
    for k, direction in enumerate(DIRECTIONS):
        exists, there = places[k]
        r0 = starts.get(direction[0], RIM + rows)
        c0 = starts.get(direction[1], RIM + columns)
        _, nr, nc, _ = recv[k].shape

        @pl.when(exists)
        def _(k=k, there=there, r0=r0, c0=c0, nr=nr, nc=nc):
            copies[k].wait_send()
            pltpu.make_async_remote_copy(
                src_ref=stage[k],
                dst_ref=recv[k],
                send_sem=send_sem.at[k],
                recv_sem=recv_sem.at[k],
                device_id=there,
                device_id_type=MESH,
            ).wait_recv()
            value = recv[k][...].astype(F32)
            for which in range(2):
                pad[which, :, r0 : r0 + nr, c0 : c0 + nc] = value[
                    which * frames : (which + 1) * frames
                ]

    def inside(depth, wide, rim):
        shape = (depth, cols, chans)
        r = lax.broadcasted_iota(jnp.int32, shape, 0) + (me[0] * rows - rim)
        c = lax.broadcasted_iota(jnp.int32, shape, 1)
        place = c + (me[1] * columns - rim)
        ok = (r >= 0) & (r < rows * grid[0]) & (place >= 0) & (place < columns * grid[1])
        return ok & (c < wide)

    s1, h1, s2, h2 = s1_ref[...], h1_ref[...], s2_ref[...], h2_ref[...]
    ok1 = inside(deep, columns + 2 * RIM, RIM)
    for t in range(frames):
        z1 = pad[0, t] * s1 + h1
        store_wide(w1, t, jnp.where(ok1, z1 * sigmoid(z1), 0.0))
        store_wide(wg, t, pad[1, t])

    loads[0].wait()
    ok2 = inside(inner, columns + 2, 1)
    for t in range(frames):
        total = jnp.zeros((inner * cols, chans), F32)
        for kt in range(max(2 - t, 0), 3):
            for kw in range(3):
                weights = jnp.concatenate([k1_ref[kt, kh, kw] for kh in range(3)], axis=0)
                total = total + dot(
                    flat2(w1[t + kt - 2, kw : kw + inner]), weights, ((1,), (0,))
                )
        z2 = (total.reshape(inner, cols, chans) + b1_ref[...]) * s2 + h2
        sig = sigmoid(z2)
        store_wide(w2, t, jnp.where(ok2, z2 * sig, 0.0))
        ds2[t] = jnp.where(ok2, sig * (1.0 + z2 * (1.0 - sig)) * s2, 0.0)

    def kernel_terms(which, wide, skip, grads):
        for kt in range(3):
            first = 2 - kt
            for kw in range(3):
                slab = wide[: frames - first, kw + skip : kw + skip + rows]
                term = dot(flat2(slab), flat2(grads[first:]), ((0,), (0,)))
                for kh in range(3):
                    at = (kt * 9 + kh * 3 + kw) * chans
                    terms[which, at : at + chans] = term[kh * chans : (kh + 1) * chans]
        bias = jnp.sum(flat2(own[which]), axis=0, keepdims=True)
        tail = terms.shape[1] - taps
        lead = lax.broadcasted_iota(jnp.int32, (tail, chans), 0) == 0
        terms[which, taps:] = jnp.where(lead, bias, 0.0)

    kernel_terms(0, w2, 0, own[0].astype(BF16))
    reducer.start(0)

    def back(wide, kernel_ref, t, depth):
        total = jnp.zeros((depth * cols, chans), F32)
        for kt in range(t, 3):
            for kw in range(3):
                weights = jnp.concatenate(
                    [kernel_ref[kt, 2 - kh, 2 - kw] for kh in range(3)], axis=1
                )
                total = total + dot(
                    flat2(wide[t + 2 - kt, kw : kw + depth]), weights, ((1,), (1,))
                )
        return total.reshape(depth, cols, chans)

    loads[1].wait()
    c = lax.broadcasted_iota(jnp.int32, (rows, cols, chans), 1)
    mine = (c >= 1) & (c <= columns)
    for t in range(frames):
        dc1 = (back(wg, k2_ref, t, inner) * ds2[t]).astype(BF16).astype(F32)
        store_wide(wd, t, dc1)
        own[1, t] = jnp.where(mine, dc1[1 : 1 + rows], 0.0)

    reducer.halves(0)
    kernel_terms(1, w1, 1, own[1].astype(BF16))
    reducer.start(1)

    def input_grad(t):
        da1 = back(wd, k1_ref, t, rows)[:, :columns]
        z1 = x_ref[t].astype(F32) * s1 + h1
        sig = sigmoid(z1)
        slope = sig * (1.0 + z1 * (1.0 - sig))
        out_ref[t] = (g_ref[t].astype(F32) + da1 * slope * s1).astype(BF16)

    input_grad(0)
    reducer.halves(1)
    reducer.parts(0)
    for t in range(1, frames):
        input_grad(t)
    reducer.pieces(0)
    reducer.parts(1)
    reducer.join_pieces(0)
    reducer.pieces(1)
    reducer.join_parts(0)
    reducer.join_pieces(1)
    reducer.join_parts(1)
    for w in range(2):
        reducer.finish(w)


def widen_kernel(taps, full, x_ref, two_ref, one_ref, bias_two_ref, bias_one_ref, y_ref):
    for w, (out_ref, bias_ref) in enumerate(((two_ref, bias_two_ref), (one_ref, bias_one_ref))):
        out_ref[...] = full[w, :taps].astype(F32)
        bias_ref[...] = full[w, taps : taps + 16].astype(F32)[0]
    y_ref[...] = x_ref[...]


def body(sizes, x, g, k1, b1, k2, s1, h1, s2, h2):
    x, g = (jnp.transpose(v, (0, 2, 1, 3)) for v in (x, g))
    frames, rows, columns, chans = x.shape
    factor = 1.0 / math.sqrt(frames * rows * sizes[1] * columns * sizes[0])
    taps = 27 * chans
    height = round_up(taps + 16, 16 * sizes[0] * sizes[1])
    cols = round_up(columns + 2 * RIM, 16)
    deep, inner = rows + 2 * RIM, rows + 2
    many_b, many_c = 2 * sizes[0], sizes[1] // 4
    half = height // 2
    part = half // many_b
    piece = part // many_c
    slots = [1, many_b - 1, many_c - 1, many_c - 1, many_b - 1, 1]
    rims = [pltpu.VMEM(rim_shape(d, frames, rows, columns, chans), BF16) for d in DIRECTIONS]
    vectors = [v.reshape(1, chans) for v in (b1, s1, h1, s2, h2)]
    hbm = pl.BlockSpec(memory_space=pl.ANY)
    grad_input, full = pl.pallas_call(
        functools.partial(block_kernel, sizes, factor),
        name="block",
        out_shape=[
            jax.ShapeDtypeStruct(x.shape, BF16),
            jax.ShapeDtypeStruct((2, height, chans), BF16),
        ],
        in_specs=[VMEM, VMEM, hbm, VMEM, hbm] + [VMEM] * 4,
        out_specs=[VMEM] * 2,
        scratch_shapes=rims
        + rims
        + [pltpu.SemaphoreType.DMA((8,)), pltpu.SemaphoreType.DMA((8,))]
        + [pltpu.SemaphoreType.DMA((2,)), pltpu.VMEM(k1.shape, BF16), pltpu.VMEM(k2.shape, BF16)]
        + [
            pltpu.VMEM((2, frames, deep, cols, chans), F32),
            pltpu.VMEM((frames, deep, cols, 3 * chans), BF16),
            pltpu.VMEM((frames, deep, cols, 3 * chans), BF16),
            pltpu.VMEM((frames, inner, cols, 3 * chans), BF16),
            pltpu.VMEM((frames, inner, cols, 3 * chans), BF16),
            pltpu.VMEM((frames, inner, cols, chans), F32),
            pltpu.VMEM((2, frames, rows, cols, chans), F32),
            pltpu.VMEM((2, height, chans), F32),
        ]
        + [
            pltpu.VMEM((2, half, chans), BF16),
            pltpu.VMEM((2, half, chans), BF16),
            pltpu.VMEM((2, half, chans), BF16),
            pltpu.VMEM((2, many_b - 1, part, chans), BF16),
            pltpu.VMEM((2, part, chans), BF16),
            pltpu.VMEM((2, many_c - 1, piece, chans), BF16),
            pltpu.VMEM((2, half, chans), F32),
        ]
        + [pltpu.SemaphoreType.DMA((2, n)) for n in slots for _ in range(2)],
        compiler_params=pltpu.CompilerParams(collective_id=0, has_side_effects=True),
    )(x, g, k1, vectors[0], k2, *vectors[1:])
    grad_two, grad_one, bias_two, bias_one, grad_input = pl.pallas_call(
        functools.partial(widen_kernel, taps),
        name="widen",
        out_shape=[jax.ShapeDtypeStruct((taps, chans), F32)] * 2
        + [jax.ShapeDtypeStruct((chans,), F32)] * 2
        + [jax.ShapeDtypeStruct(x.shape, BF16)],
        in_specs=[VMEM] * 2,
        out_specs=[VMEM] * 5,
    )(full, grad_input)
    return (
        jnp.transpose(grad_input, (0, 2, 1, 3)),
        grad_one.reshape(k1.shape),
        bias_one,
        grad_two.reshape(k2.shape),
        bias_two,
    )


def solution(mesh):
    sizes = (mesh.shape["ha"], mesh.shape["wa"])
    cells = P(None, "ha", "wa", None)
    return jax.shard_map(
        functools.partial(body, sizes),
        mesh=mesh,
        in_specs=(cells, cells) + (P(),) * 7,
        out_specs=(cells, P(), P(), P(), P()),
        check_vma=False,
    )
```

time: 283 us -> 52.2 us (0.18)
  waiting for transfers between devices: 90.6 us -> 0 us
  local copies, waits for them, and re-layouts: 62.4 us -> 0 us
  Pallas kernels: 0 us -> 51.4 us
  blocking collectives: 45 us -> 0 us
  starting transfers between devices: 31 us -> 0 us
  matrix products: 24.2 us -> 0 us
  between operations: 15.4 us -> 0.64 us
  other arithmetic: 12.8 us -> 0 us
    psum x1 -> x0, waiting for transfers between devices: 88.1 us -> none  [body(): lax.psum((grad_one, bias_a, grad_two, bias_b), ('ha', 'wa'))]
    pallas_call x0 -> x2, Pallas kernels: none -> 51.4 us  [the longest x1 47.9 us: body(): pl.pallas_call(functools.partial(block_kernel, sizes, factor), name='bloc...]
    psum x1 -> x0, blocking collectives: 45 us -> none  [body(): lax.psum((grad_one, bias_a, grad_two, bias_b), ('ha', 'wa'))]
    ppermute x12 -> x0, starting transfers between devices: 31 us -> none  [the longest x6 23.3 us: with_halo(): lax.ppermute(tail, axis, [(i, (i + 1) % count) for i in range(ends)])]
    slice x38 -> x0, local copies, waits for them, and re-layouts: 31 us -> none  [the longest x30 25.2 us: convolve(): wide[step_t:step_t + frames, step_h:step_h + rows].reshape(-1, 3 * inner)]
    reshape x30 -> x0, local copies, waits for them, and re-layouts: 25.4 us -> none  [the longest x27 25.2 us: convolve(): wide[step_t:step_t + frames, step_h:step_h + rows].reshape(-1, 3 * inner)]
    dot_general x45 -> x0, matrix products: 24.2 us -> none  [the longest x27 17.8 us: convolve(): jnp.dot(slab, kernel[step_t, step_h].reshape(3 * inner, -1), preferred_el...]
    unnamed x118 -> x0, local copies, waits for them, and re-layouts: 5.83 us -> none
  transfers between devices with their start and end apart: 13 -> 0, of which waited for: 2 -> 0; matrix products, arithmetic and copies ran while one was open for 12% -> 0% of each run, Pallas kernels for 0% -> 0%
where the time goes in v2:
time: 52.2 us; the launch traced here: 52 us
  Pallas kernels  51.4 us (98%)
  between operations  0.64 us (1%)
    pallas_call x1, Pallas kernels, body(): pl.pallas_call(functools.partial(block_kernel, sizes, factor), name='bloc...  47.9 us
    pallas_call x1, Pallas kernels, body(): pl.pallas_call(functools.partial(widen_kernel, taps), name='widen', out_s...  3.46 us

profile of v2, /device:TPU:0, one launch (start us, length us, event | category | flops | bytes accessed | tf_op | source)
XLA Modules:
  0.0 52.0 jit_solution(8826547632418426296)
XLA Ops:
  0.6 47.9 %block.1 = (bf16[3,10,23,128]{3,2,1,0:T(8,128)(2,1)}, bf16[2,3584,128]{2,1,0:T(8,128)(2,1)}) custom-call(bf16[3,10,23,128]{3,2,1,0:T(8,128)(2,1)} %bitcast.10, bf16[3,10,23,128]{3,2,1,0:T(8,128)(2,1)} %bitcast.11, bf16[3,3,3,128,128]{4,3,2,1,0:T(8,128)(2,1)} %k1_hbm.1, f32[1,128]{1,0:T(1,128)} %bitcast.12, bf16[3,3,3,128,128]{4,3,2,1,0:T(8,128)(2,1)} %k2_hbm.1, ...), custom_call_target="tpu_custom_call" | custom-call | tf_op jit(solution)/shard_map/block/pallas_call | solution.py:390
  48.5 3.5 %widen.1 = (f32[3456,128]{1,0:T(8,128)}, f32[3456,128]{1,0:T(8,128)}, f32[128]{0:T(128)}, f32[128]{0:T(128)}, bf16[3,10,23,128]{3,2,1,0:T(8,128)(2,1)}) custom-call(bf16[2,3584,128]{2,1,0:T(8,128)(2,1)} %get-tuple-element.12.full, bf16[3,10,23,128]{3,2,1,0:T(8,128)(2,1)} %get-tuple-element.13.x_ref), custom_call_target="tpu_custom_call" | custom-call | tf_op jit(solution)/shard_map/widen/pallas_call | solution.py:425

commit v3 on v2

--- a/solution.py
+++ b/solution.py
@@ -14,6 +14,7 @@
 VMEM = pl.BlockSpec(memory_space=pltpu.VMEM)
 DIRECTIONS = [(dy, dx) for dy in (-1, 0, 1) for dx in (-1, 0, 1) if (dy, dx) != (0, 0)]
 RIM = 2
+GROUPS = 2
 
 
 def span(step, size):
@@ -61,7 +62,7 @@
 
 
 def rows_at(start, size):
-    return pl.ds(pl.multiple_of(start, 16), size)
+    return pl.ds(pl.multiple_of(start, 8), size)
 
 
 class Reducer:
@@ -300,6 +301,16 @@
         store_wide(w2, t, jnp.where(ok2, z2 * sig, 0.0))
         ds2[t] = jnp.where(ok2, sig * (1.0 + z2 * (1.0 - sig)) * s2, 0.0)
 
+    def put(which, at, value):
+        size = terms.shape[1]
+        end = at + value.shape[0]
+        for k in range(GROUPS):
+            low, high = max(at, k * size), min(end, (k + 1) * size)
+            if low < high:
+                terms[which * GROUPS + k, low - k * size : high - k * size] = value[
+                    low - at : high - at
+                ]
+
     def kernel_terms(which, wide, skip, grads):
         for kt in range(3):
             first = 2 - kt
@@ -308,14 +319,15 @@
                 term = dot(flat2(slab), flat2(grads[first:]), ((0,), (0,)))
                 for kh in range(3):
                     at = (kt * 9 + kh * 3 + kw) * chans
-                    terms[which, at : at + chans] = term[kh * chans : (kh + 1) * chans]
+                    put(which, at, term[kh * chans : (kh + 1) * chans])
         bias = jnp.sum(flat2(own[which]), axis=0, keepdims=True)
-        tail = terms.shape[1] - taps
+        tail = GROUPS * terms.shape[1] - taps
         lead = lax.broadcasted_iota(jnp.int32, (tail, chans), 0) == 0
-        terms[which, taps:] = jnp.where(lead, bias, 0.0)
+        put(which, taps, jnp.where(lead, bias, 0.0))
 
     kernel_terms(0, w2, 0, own[0].astype(BF16))
     reducer.start(0)
+    reducer.start(1)
 
     def back(wide, kernel_ref, t, depth):
         total = jnp.zeros((depth * cols, chans), F32)
@@ -338,8 +350,10 @@
         own[1, t] = jnp.where(mine, dc1[1 : 1 + rows], 0.0)
 
     reducer.halves(0)
+    reducer.halves(1)
     kernel_terms(1, w1, 1, own[1].astype(BF16))
-    reducer.start(1)
+    reducer.start(2)
+    reducer.start(3)
 
     def input_grad(t):
         da1 = back(wd, k1_ref, t, rows)[:, :columns]
@@ -349,18 +363,27 @@
         out_ref[t] = (g_ref[t].astype(F32) + da1 * slope * s1).astype(BF16)
 
     input_grad(0)
-    reducer.halves(1)
+    reducer.halves(2)
+    reducer.halves(3)
     reducer.parts(0)
-    for t in range(1, frames):
-        input_grad(t)
+    input_grad(1)
+    reducer.parts(1)
+    input_grad(2)
     reducer.pieces(0)
-    reducer.parts(1)
+    reducer.pieces(1)
+    reducer.parts(2)
     reducer.join_pieces(0)
-    reducer.pieces(1)
+    reducer.parts(3)
+    reducer.join_pieces(1)
+    reducer.pieces(2)
+    reducer.pieces(3)
     reducer.join_parts(0)
-    reducer.join_pieces(1)
     reducer.join_parts(1)
-    for w in range(2):
+    reducer.join_pieces(2)
+    reducer.join_pieces(3)
+    reducer.join_parts(2)
+    reducer.join_parts(3)
+    for w in range(2 * GROUPS):
         reducer.finish(w)
 
 
@@ -376,13 +399,14 @@
     frames, rows, columns, chans = x.shape
     factor = 1.0 / math.sqrt(frames * rows * sizes[1] * columns * sizes[0])
     taps = 27 * chans
-    height = round_up(taps + 16, 16 * sizes[0] * sizes[1])
+    height = round_up(taps + 16, 8 * GROUPS * sizes[0] * sizes[1]) // GROUPS
     cols = round_up(columns + 2 * RIM, 16)
     deep, inner = rows + 2 * RIM, rows + 2
     many_b, many_c = 2 * sizes[0], sizes[1] // 4
     half = height // 2
     part = half // many_b
     piece = part // many_c
+    many = 2 * GROUPS
     slots = [1, many_b - 1, many_c - 1, many_c - 1, many_b - 1, 1]
     rims = [pltpu.VMEM(rim_shape(d, frames, rows, columns, chans), BF16) for d in DIRECTIONS]
     vectors = [v.reshape(1, chans) for v in (b1, s1, h1, s2, h2)]
@@ -392,7 +416,7 @@
         name="block",
         out_shape=[
             jax.ShapeDtypeStruct(x.shape, BF16),
-            jax.ShapeDtypeStruct((2, height, chans), BF16),
+            jax.ShapeDtypeStruct((many, height, chans), BF16),
         ],
         in_specs=[VMEM, VMEM, hbm, VMEM, hbm] + [VMEM] * 4,
         out_specs=[VMEM] * 2,
@@ -408,18 +432,18 @@
             pltpu.VMEM((frames, inner, cols, 3 * chans), BF16),
             pltpu.VMEM((frames, inner, cols, chans), F32),
             pltpu.VMEM((2, frames, rows, cols, chans), F32),
-            pltpu.VMEM((2, height, chans), F32),
+            pltpu.VMEM((many, height, chans), F32),
         ]
         + [
-            pltpu.VMEM((2, half, chans), BF16),
-            pltpu.VMEM((2, half, chans), BF16),
-            pltpu.VMEM((2, half, chans), BF16),
-            pltpu.VMEM((2, many_b - 1, part, chans), BF16),
-            pltpu.VMEM((2, part, chans), BF16),
-            pltpu.VMEM((2, many_c - 1, piece, chans), BF16),
-            pltpu.VMEM((2, half, chans), F32),
+            pltpu.VMEM((many, half, chans), BF16),
+            pltpu.VMEM((many, half, chans), BF16),
+            pltpu.VMEM((many, half, chans), BF16),
+            pltpu.VMEM((many, many_b - 1, part, chans), BF16),
+            pltpu.VMEM((many, part, chans), BF16),
+            pltpu.VMEM((many, many_c - 1, piece, chans), BF16),
+            pltpu.VMEM((many, half, chans), F32),
         ]
-        + [pltpu.SemaphoreType.DMA((2, n)) for n in slots for _ in range(2)],
+        + [pltpu.SemaphoreType.DMA((many, n)) for n in slots for _ in range(2)],
         compiler_params=pltpu.CompilerParams(collective_id=0, has_side_effects=True),
     )(x, g, k1, vectors[0], k2, *vectors[1:])
     grad_two, grad_one, bias_two, bias_one, grad_input = pl.pallas_call(
@@ -430,7 +454,7 @@
         + [jax.ShapeDtypeStruct(x.shape, BF16)],
         in_specs=[VMEM] * 2,
         out_specs=[VMEM] * 5,
-    )(full, grad_input)
+    )(full.reshape(2, GROUPS * height, chans), grad_input)
     return (
         jnp.transpose(grad_input, (0, 2, 1, 3)),
         grad_one.reshape(k1.shape),

time: 52.2 us -> 49.2 us (0.943)
  Pallas kernels: 51.4 us -> 48.4 us
    pallas_call x1, Pallas kernels: 47.9 us -> 45 us  [body(): pl.pallas_call(functools.partial(block_kernel, sizes, factor), name='bloc...]
where the time goes in v3:
time: 49.2 us; the launch traced here: 49.1 us
  Pallas kernels  48.4 us (98%)
  between operations  0.64 us (1%)
    pallas_call x1, Pallas kernels, body(): pl.pallas_call(functools.partial(block_kernel, sizes, factor), name='bloc...  45 us
    pallas_call x1, Pallas kernels, body(): pl.pallas_call(functools.partial(widen_kernel, taps), name='widen', out_s...  3.46 us

profile of v3, /device:TPU:0, one launch (start us, length us, event | category | flops | bytes accessed | tf_op | source)
XLA Modules:
  0.0 49.1 jit_solution(16226921931984655037)
XLA Ops:
  0.6 45.0 %block.1 = (bf16[3,10,23,128]{3,2,1,0:T(8,128)(2,1)}, bf16[4,1792,128]{2,1,0:T(8,128)(2,1)}) custom-call(bf16[3,10,23,128]{3,2,1,0:T(8,128)(2,1)} %bitcast.12, bf16[3,10,23,128]{3,2,1,0:T(8,128)(2,1)} %bitcast.13, bf16[3,3,3,128,128]{4,3,2,1,0:T(8,128)(2,1)} %k1_hbm.1, f32[1,128]{1,0:T(1,128)} %bitcast.14, bf16[3,3,3,128,128]{4,3,2,1,0:T(8,128)(2,1)} %k2_hbm.1, ...), custom_call_target="tpu_custom_call" | custom-call | tf_op jit(solution)/shard_map/block/pallas_call | solution.py:414
  45.6 3.5 %widen.1 = (f32[3456,128]{1,0:T(8,128)}, f32[3456,128]{1,0:T(8,128)}, f32[128]{0:T(128)}, f32[128]{0:T(128)}, bf16[3,10,23,128]{3,2,1,0:T(8,128)(2,1)}) custom-call(bf16[2,3584,128]{2,1,0:T(8,128)(2,1)} %bitcast.11, bf16[3,10,23,128]{3,2,1,0:T(8,128)(2,1)} %get-tuple-element.13.x_ref), custom_call_target="tpu_custom_call" | custom-call | tf_op jit(solution)/shard_map/widen/pallas_call | solution.py:449

commit v4 on v3

--- a/solution.py
+++ b/solution.py
@@ -158,16 +158,21 @@
     def spread(self, w, here, stage, j, there):
         self.send(self.full.at[w, here], self.full.at[w, here], stage, w, j - 1, there)
 
+    def part_rows(self, q):
+        return rows_at(self.core * self.half + q * self.part, self.part)
+
     def join_pieces(self, w):
         self.arrive(3, w)
-        here = rows_at(self.core * self.half + self.b * self.part, self.part)
+        here = self.part_rows(self.b)
         for j in range(1, self.many_b):
             self.spread(w, here, 4, j, self.in_b(j)[1])
+        self.spread(w, here, 5, 1, self.partner)
 
     def join_parts(self, w):
-        self.arrive(4, w)
-        here = rows_at(self.core * self.half, self.half)
-        self.spread(w, here, 5, 1, self.partner)
+        for j in range(1, self.many_b):
+            self.copies[4, w][j - 1].wait_recv()
+            here = self.part_rows(lax.rem(self.b + self.many_b - j, self.many_b))
+            self.spread(w, here, 5, j + 1, self.partner)
 
     def finish(self, w):
         self.arrive(5, w)
@@ -407,7 +412,7 @@
     part = half // many_b
     piece = part // many_c
     many = 2 * GROUPS
-    slots = [1, many_b - 1, many_c - 1, many_c - 1, many_b - 1, 1]
+    slots = [1, many_b - 1, many_c - 1, many_c - 1, many_b - 1, many_b]
     rims = [pltpu.VMEM(rim_shape(d, frames, rows, columns, chans), BF16) for d in DIRECTIONS]
     vectors = [v.reshape(1, chans) for v in (b1, s1, h1, s2, h2)]
     hbm = pl.BlockSpec(memory_space=pl.ANY)

time: 49.2 us -> 49.2 us (level)
  no operation moved by 1% of the time
where the time goes in v4:
time: 49.2 us; the launch traced here: 49.1 us
  Pallas kernels  48.4 us (98%)
  between operations  0.64 us (1%)
    pallas_call x1, Pallas kernels, body(): pl.pallas_call(functools.partial(block_kernel, sizes, factor), name='bloc...  44.9 us
    pallas_call x1, Pallas kernels, body(): pl.pallas_call(functools.partial(widen_kernel, taps), name='widen', out_s...  3.46 us

profile of v4, /device:TPU:0, one launch (start us, length us, event | category | flops | bytes accessed | tf_op | source)
XLA Modules:
  0.0 49.1 jit_solution(17517309049715101868)
XLA Ops:
  0.6 44.9 %block.1 = (bf16[3,10,23,128]{3,2,1,0:T(8,128)(2,1)}, bf16[4,1792,128]{2,1,0:T(8,128)(2,1)}) custom-call(bf16[3,10,23,128]{3,2,1,0:T(8,128)(2,1)} %bitcast.12, bf16[3,10,23,128]{3,2,1,0:T(8,128)(2,1)} %bitcast.13, bf16[3,3,3,128,128]{4,3,2,1,0:T(8,128)(2,1)} %k1_hbm.1, f32[1,128]{1,0:T(1,128)} %bitcast.14, bf16[3,3,3,128,128]{4,3,2,1,0:T(8,128)(2,1)} %k2_hbm.1, ...), custom_call_target="tpu_custom_call" | custom-call | tf_op jit(solution)/shard_map/block/pallas_call | solution.py:419
  45.6 3.5 %widen.1 = (f32[3456,128]{1,0:T(8,128)}, f32[3456,128]{1,0:T(8,128)}, f32[128]{0:T(128)}, f32[128]{0:T(128)}, bf16[3,10,23,128]{3,2,1,0:T(8,128)(2,1)}) custom-call(bf16[2,3584,128]{2,1,0:T(8,128)(2,1)} %bitcast.11, bf16[3,10,23,128]{3,2,1,0:T(8,128)(2,1)} %get-tuple-element.13.x_ref), custom_call_target="tpu_custom_call" | custom-call | tf_op jit(solution)/shard_map/widen/pallas_call | solution.py:454
